TPU v7x, 32 devices: a whole 2x2x4 slice. The times are simulated.
32 devices in a mesh: groups: 2 (over x), rows: 16 (over z, y, core).
Axes of the slice: x: 2, y: 2, z: 4, core: 2. Of those that a mesh axis runs over, the one named last changes fastest.
Arguments:
- features: float32 [448, 14, 192], P(('groups', 'rows')), parts along dimension 0, may hold values from -6 to 6
- fine_gain_one: float32 [192], replicated, may hold values from 0.1 to 1.9
- fine_project_in: float32 [192, 576], replicated, may hold values from -30 to 30
- fine_project_out: float32 [192, 192], replicated, may hold values from -0.4375 to 0.4375
- fine_gain_two: float32 [192], replicated, may hold values from 0.1 to 1.9
- fine_expand: float32 [192, 768], replicated, may hold values from -0.4375 to 0.4375
- fine_contract: float32 [768, 192], replicated, may hold values from -0.21875 to 0.21875
- merge_gain: float32 [768], replicated, may hold values from 0.1 to 1.9
- merge_weight: float32 [768, 384], replicated, may hold values from -0.21875 to 0.21875
- coarse_gain: float32 [384], replicated, may hold values from 0.1 to 1.9
- coarse_project_in: float32 [384, 1152], replicated, may hold values from -30 to 30
- coarse_project_out: float32 [384, 384], replicated, may hold values from -0.3125 to 0.3125
- cotangent: float32 [224, 7, 384], P(('groups', 'rows')), parts along dimension 0, may hold values from -6 to 6
Outputs:
- coarse_out: float32 [224, 7, 384], P(('groups', 'rows')), parts along dimension 0
- gradient_features: float32 [448, 14, 192], P(('groups', 'rows')), parts along dimension 0
- gradient_fine_gain_one: float32 [384], P('groups'), parts along dimension 0
- gradient_fine_project_in: float32 [384, 576], P('groups'), parts along dimension 0
- gradient_fine_project_out: float32 [384, 192], P('groups'), parts along dimension 0
- gradient_fine_gain_two: float32 [384], P('groups'), parts along dimension 0
- gradient_fine_expand: float32 [384, 768], P('groups'), parts along dimension 0
- gradient_fine_contract: float32 [1536, 192], P('groups'), parts along dimension 0
- gradient_merge_gain: float32 [1536], P('groups'), parts along dimension 0
- gradient_merge_weight: float32 [1536, 384], P('groups'), parts along dimension 0
- gradient_coarse_gain: float32 [768], P('groups'), parts along dimension 0
- gradient_coarse_project_in: float32 [768, 1152], P('groups'), parts along dimension 0
- gradient_coarse_project_out: float32 [768, 384], P('groups'), parts along dimension 0
There are 2 independent parts, one for each index of `groups`. A program takes and returns all parts, laid end to end along the dimension named above; an argument that names none is the same for every part. Nothing has to cross between parts.
All inputs are finite; a program needn't handle non-finite values.
Results may differ from a plain program's by a relative error of at most 0.0004.
Values sent between devices are 32-bit elements; how exact they have to be, the bound alone decides.
A program may use at most 128 MiB of HBM per device.

v0:
```python
import functools

import jax
import jax.numpy as jnp
from jax import lax
from jax.experimental import pallas as pl
from jax.experimental.pallas import tpu as pltpu
from jax.sharding import PartitionSpec as P

HEAD_DIM = 32
WIN = 7
PAD = 8
TOK = PAD * PAD
SHIFT = 3
EPSILON = 1e-05
MESH = pl.DeviceIdType.MESH
F32 = jnp.float32
BF16 = jnp.bfloat16
NN = (((1,), (0,)), ((), ()))
NT = (((1,), (1,)), ((), ()))
TN = (((0,), (0,)), ((), ()))


def halves(a):
    hi = a.astype(BF16)
    return hi, (a - hi.astype(F32)).astype(BF16)


def mm(a, b, dims=NN):
    a = a if isinstance(a, tuple) else halves(a)
    b = b if isinstance(b, tuple) else halves(b)
    dot = functools.partial(lax.dot_general, dimension_numbers=dims, preferred_element_type=F32)
    return dot(a[0], b[0]) + (dot(a[0], b[1]) + dot(a[1], b[0]))


def runs(first, count, breadth):
    head = min(count, breadth - first % breadth)
    pieces = [(0, first % breadth, head)]
    return pieces + ([(head, 0, count - head)] if head < count else [])


def take_windows(dst, first_rows, slab_ref, skip, last_rows, win_cols):
    breadth = slab_ref.shape[1]
    sources = [(r, i) for r in (first_rows,) if r is not None for i in range(r.shape[0])]
    sources += [(slab_ref, i) for i in range(skip, slab_ref.shape[0])]
    sources += [(r, i) for r in (last_rows,) if r is not None for i in range(r.shape[0])]
    dst[...] = jnp.zeros_like(dst)
    for w in range(dst.shape[0]):
        row, col = divmod(w, win_cols)
        for i in range(WIN):
            ref, at = sources[row * WIN + i]
            for place, start, size in runs(col * WIN + SHIFT, WIN, breadth):
                dst[w, i, place : place + size, :] = ref[at, start : start + size, :]


def put_windows(dst, src, win_cols):
    breadth = dst.shape[1]
    for w in range(src.shape[0]):
        row, col = divmod(w, win_cols)
        for place, start, size in runs(col * WIN + SHIFT, WIN, breadth):
            dst[row * WIN : (row + 1) * WIN, start : start + size, :] = src[
                w, :WIN, place : place + size, :
            ]


def norm(v):
    centered = v - jnp.mean(v, axis=-1, keepdims=True)
    scale = lax.rsqrt(jnp.mean(centered * centered, axis=-1, keepdims=True) + EPSILON)
    return centered * scale, scale


def norm_back(dn, n, scale):
    return scale * (
        dn - jnp.mean(dn, axis=-1, keepdims=True) - n * jnp.mean(dn * n, axis=-1, keepdims=True)
    )


def spread(a, heads):
    lane = lax.broadcasted_iota(jnp.int32, a.shape, 1) // HEAD_DIM
    return jnp.concatenate([jnp.where(lane == h, a, 0.0) for h in range(heads)], axis=0)


def gather_heads(a, heads):
    rows = a.shape[0] // heads
    lane = lax.broadcasted_iota(jnp.int32, (rows, a.shape[1]), 1) // HEAD_DIM
    total = jnp.where(lane == 0, a[:rows], 0.0)
    for h in range(1, heads):
        total = jnp.where(lane == h, a[h * rows : (h + 1) * rows], total)
    return total


def allowed(last_row, last_col):
    def label(axis):
        t = lax.broadcasted_iota(jnp.int32, (TOK, TOK), axis)
        r, c = t // PAD, t % PAD
        lab = jnp.where(r >= WIN - SHIFT, last_row * 2, 0) + jnp.where(
            c >= WIN - SHIFT, last_col, 0
        )
        return lab, (r < WIN) & (c < WIN)

    lq, _ = label(0)
    lk, real = label(1)
    return (lq == lk) & real


def attend(q, k, v, mask, heads):
    s = mm(spread(q, heads), k, NT) * HEAD_DIM**-0.5
    s = jnp.where(jnp.concatenate([mask] * heads, axis=0), s, -1e30)
    w = jnp.exp(s - jnp.max(s, axis=-1, keepdims=True))
    w = w / jnp.sum(w, axis=-1, keepdims=True)
    return w, gather_heads(mm(w, v), heads)


def attend_back(dctx, q, k, v, w, heads):
    dc = halves(spread(dctx, heads))
    dw = mm(dc, v, NT)
    dv = mm(w, dc, TN)
    ds = w * (dw - jnp.sum(dw * w, axis=-1, keepdims=True)) * HEAD_DIM**-0.5
    ds = halves(ds)
    dq = gather_heads(mm(ds, k), heads)
    dk = mm(ds, spread(q, heads), TN)
    return dq, dk, dv


def fine_forward(
    win_cols, last_ref, f_ref, halo_ref, g_ref, win_ref, wout_ref, mid_ref, head_ref, x_ref, qkv_ref, w_ref, ctx_ref, cells
):
    channels = x_ref.shape[1]
    heads = channels // HEAD_DIM
    windows = cells.shape[0]
    take_windows(cells, None, f_ref, SHIFT, halo_ref, win_cols)
    x = cells[...].reshape(windows * TOK, channels)
    x_ref[...] = x
    n, _ = norm(x)
    u = halves(n * g_ref[...])
    parts = []
    for part in range(3):
        got = mm(u, win_ref[:, part * channels : (part + 1) * channels])
        qkv_ref[part] = got
        parts.append(got)
    for i in range(windows):
        row, col = divmod(i, win_cols)
        bottom = last_ref[0] if row == windows // win_cols - 1 else 0
        mask = allowed(bottom, int(col == win_cols - 1))
        at = slice(i * TOK, (i + 1) * TOK)
        w, ctx = attend(parts[0][at], parts[1][at], parts[2][at], mask, heads)
        w_ref[i] = w
        ctx_ref[at, :] = ctx
    mid = x + mm(ctx_ref[...], wout_ref[...])
    cells[...] = mid.reshape(cells.shape)
    put_windows(mid_ref, cells, win_cols)
    head_ref[...] = mid_ref[:SHIFT]


def fine_backward(
    grad_scale, first, win_cols, d_ref, prefix_ref, x_ref, g_ref, win_ref, wout_ref, qkv_ref, w_ref, ctx_ref, _, dx_ref, tail_ref, pack_ref, own, cells, sem
):
    channels = x_ref.shape[1]
    heads = channels // HEAD_DIM
    windows = x_ref.shape[0] // TOK
    take_windows(cells, prefix_ref, d_ref, 0, None, win_cols)
    d = cells[...].reshape(x_ref.shape)
    n, scale = norm(x_ref[...])
    g = g_ref[...]
    u = halves(n * g)
    dh = halves(d)
    dctx = mm(dh, wout_ref[...], NT)
    dwout = mm(ctx_ref[...], dh, TN)
    grads = ([], [], [])
    for i in range(windows):
        at = slice(i * TOK, (i + 1) * TOK)
        got = attend_back(dctx[at], qkv_ref[0, at], qkv_ref[1, at], qkv_ref[2, at], w_ref[i], heads)
        for group, part in zip(grads, got):
            group.append(part)
    du = 0.0
    weight = []
    for part in range(3):
        dp = halves(jnp.concatenate(grads[part], axis=0))
        du += mm(dp, win_ref[:, part * channels : (part + 1) * channels], NT)
        weight.append(mm(u, dp, TN) * grad_scale)
    own[:channels, :] = jnp.concatenate(weight[:2], axis=1)
    own[channels : 2 * channels, :] = jnp.concatenate([weight[2], dwout * grad_scale], axis=1)
    own[2 * channels :, :] = jnp.zeros_like(own[2 * channels :, :])
    own[2 * channels : 2 * channels + 1, :channels] = (
        jnp.sum(du * n, axis=0, keepdims=True) * grad_scale
    )
    copy = pltpu.make_async_copy(own, pack_ref.at[pl.ds(first, own.shape[0])], sem)
    copy.start()
    cells[...] = (d + norm_back(du * g, n, scale)).reshape(cells.shape)
    put_windows(dx_ref, cells, win_cols)
    tail_ref[...] = dx_ref[dx_ref.shape[0] - SHIFT :]
    copy.wait()


def middle(
    grad_scale,
    spot,
    last_ref,
    mid_ref,
    halo_ref,
    cotangent_ref,
    cot_halo_ref,
    g2_ref,
    we_ref,
    wc_ref,
    gm_ref,
    wm_ref,
    gc_ref,
    win_ref,
    wout_ref,
    out_ref,
    out_tail_ref,
    dmid_ref,
    dmid_tail_ref,
    pack_ref,
    h_ref,
    act_ref,
    quads,
    cells,
):
    height, breadth, cf = mid_ref.shape
    cc = cotangent_ref.shape[2]
    heads = cc // HEAD_DIM
    quads[...] = jnp.zeros_like(quads)
    for k in range(4):
        dj, di = divmod(k, 2)
        for i in range(WIN):
            r = SHIFT + 2 * i + di
            ref, r = (mid_ref, r) if r < height else (halo_ref, r - height)
            for j in range(WIN):
                at = (2 * (SHIFT + j) + dj) % breadth
                quads[k, i, j : j + 1, :] = ref[r, at : at + 1, :]
    x = quads[...].reshape(4 * TOK, cf)
    n2, r2 = norm(x)
    g2 = g2_ref[...]
    u2 = halves(n2 * g2)
    h = mm(u2, we_ref[...])
    h_ref[...] = h
    act = h * (0.5 * (1.0 + lax.erf(h * 0.5**0.5)))
    act_ref[...] = act
    y = x + mm(act, wc_ref[...], NT)
    ys = [y[k * TOK : (k + 1) * TOK] for k in range(4)]
    wide = 1.0 / (4 * cf)
    mean = sum(jnp.sum(v, axis=-1, keepdims=True) for v in ys) * wide
    ys = [v - mean for v in ys]
    rm = lax.rsqrt(sum(jnp.sum(v * v, axis=-1, keepdims=True) for v in ys) * wide + EPSILON)
    nm = [v * rm for v in ys]
    gm = [gm_ref[k : k + 1, :] for k in range(4)]
    um = [halves(nm[k] * gm[k]) for k in range(4)]
    merged = sum(mm(um[k], wm_ref[k * cf : (k + 1) * cf, :]) for k in range(4))
    nc, rc = norm(merged)
    gc = gc_ref[...]
    uc = halves(nc * gc)
    q, k_, v_ = (mm(uc, win_ref[:, p * cc : (p + 1) * cc]) for p in range(3))
    w, ctx = attend(q, k_, v_, allowed(last_ref[0], 1), heads)
    cells[0] = (merged + mm(ctx, wout_ref[...])).reshape(PAD, PAD, cc)
    put_windows(out_ref, cells, 1)
    out_tail_ref[...] = out_ref[WIN - SHIFT :]
    take_windows(cells, None, cotangent_ref, SHIFT, cot_halo_ref, 1)
    cot = cells[0].reshape(TOK, cc)
    ch = halves(cot)
    pack_ref[spot["coarse_out"] : spot["coarse_out"] + cc, :] = mm(ctx, ch, TN) * grad_scale
    dctx = mm(ch, wout_ref[...], NT)
    got = attend_back(dctx, q, k_, v_, w, heads)
    du = 0.0
    for p in range(3):
        dp = halves(got[p])
        top = spot["coarse_in"] + p * cc
        pack_ref[top : top + cc, :] = mm(uc, dp, TN) * grad_scale
        du += mm(dp, win_ref[:, p * cc : (p + 1) * cc], NT)
    gains = spot["gains"]
    pack_ref[gains:, :] = jnp.zeros_like(pack_ref[gains:, :])
    pack_ref[gains + 3 : gains + 4, :] = jnp.sum(du * nc, axis=0, keepdims=True) * grad_scale
    dm = cot + norm_back(du * gc, nc, rc)
    mh = halves(dm)
    dn = []
    for k in range(4):
        top = spot["merge"] + k * cf
        pack_ref[top : top + cf, :] = mm(um[k], mh, TN) * grad_scale
        dk = mm(mh, wm_ref[k * cf : (k + 1) * cf, :], NT)
        row = gains + 1 + k // 2
        pack_ref[row : row + 1, (k % 2) * cf : (k % 2 + 1) * cf] = jnp.sum(dk * nm[k], axis=0, keepdims=True) * grad_scale
        dn.append(dk * gm[k])
    m1 = sum(jnp.sum(v, axis=-1, keepdims=True) for v in dn) * wide
    m2 = sum(jnp.sum(dn[k] * nm[k], axis=-1, keepdims=True) for k in range(4)) * wide
    dy = jnp.concatenate([rm * (dn[k] - m1 - nm[k] * m2) for k in range(4)], axis=0)
    yh = halves(dy)
    dwc = mm(yh, act_ref[...], TN) * grad_scale
    top = spot["contract"]
    for p in range(dwc.shape[1] // cc):
        pack_ref[top + p * cf : top + (p + 1) * cf, :] = dwc[:, p * cc : (p + 1) * cc]
    h = h_ref[...]
    slope = 0.5 * (1.0 + lax.erf(h * 0.5**0.5)) + h * (jnp.exp(-0.5 * h * h) * 0.3989422804014327)
    dh = halves(mm(yh, wc_ref[...]) * slope)
    dwe = mm(u2, dh, TN) * grad_scale
    top = spot["expand"]
    for p in range(dwe.shape[1] // cc):
        pack_ref[top + p * cf : top + (p + 1) * cf, :] = dwe[:, p * cc : (p + 1) * cc]
    du2 = mm(dh, we_ref[...], NT)
    pack_ref[gains : gains + 1, :cf] = jnp.sum(du2 * n2, axis=0, keepdims=True) * grad_scale
    quads[...] = (dy + norm_back(du2 * g2, n2, r2)).reshape(quads.shape)
    for k in range(4):
        dj, di = divmod(k, 2)
        for i in range(WIN):
            for j in range(WIN):
                at = (2 * (SHIFT + j) + dj) % breadth
                dmid_ref[2 * i + di, at : at + 1, :] = quads[k, i, j : j + 1, :]
    dmid_tail_ref[...] = dmid_ref[height - SHIFT :]


STREAMS = 4


def ring_sum(
    chips, seg, g_ref, out_ref, pair_buf, acc, ring_buf, pair_send, pair_recv, rs_send, rs_recv, ag_send, ag_recv, back_send, back_recv
):
    me = lax.axis_index("rows")
    core, chip = me % 2, me // 2
    column, line = chip % 2, chip // 2
    at = jnp.where(column == 0, line, chips - 1 - line)
    step = 1 - 2 * core
    sub = seg // STREAMS

    def device(q):
        q = (q + chips) % chips
        return jnp.where(q < chips // 2, q * 2, (chips - 1 - q) * 2 + 1) * 2 + core

    ahead, behind, mate = device(at + step), device(at - step), me + 1 - 2 * core
    barrier = pltpu.get_barrier_semaphore()
    for other in (ahead, behind, mate):
        pl.semaphore_signal(barrier, inc=1, device_id={"rows": other}, device_id_type=MESH)
    pl.semaphore_wait(barrier, 3)

    def slot(chunk, a):
        chunk = (chunk + 2 * chips) % chips
        return pl.ds(pl.multiple_of(chunk * seg + a * sub, 8), sub)

    def rows(half, chunk, a):
        chunk = (chunk + 2 * chips) % chips
        return pl.ds(pl.multiple_of((half * chips + chunk) * seg + a * sub, 8), sub)

    def remote(src, dst, send, recv, target):
        return pltpu.make_async_remote_copy(
            src_ref=src,
            dst_ref=dst,
            send_sem=send,
            recv_sem=recv,
            device_id={"rows": target},
            device_id_type=MESH,
        )

    def pair_copy(s, a):
        chunk = at + step * s
        return remote(
            g_ref.at[rows(1 - core, chunk, a)],
            pair_buf.at[slot(chunk, a)],
            pair_send.at[s, a],
            pair_recv.at[s, a],
            mate,
        )

    def pair_arrival(s, a):
        chunk = at - step * s
        return remote(
            g_ref.at[rows(1 - core, chunk, a)],
            pair_buf.at[slot(chunk, a)],
            pair_send.at[s, a],
            pair_recv.at[s, a],
            mate,
        )

    def rs_copy(s, a):
        return remote(
            acc.at[slot(at - step * s, a)],
            ring_buf.at[s, pl.ds(a * sub, sub)],
            rs_send.at[s, a],
            rs_recv.at[s, a],
            ahead,
        )

    def ag_copy(s, a):
        where = rows(core, at + step - step * s, a)
        return remote(out_ref.at[where], out_ref.at[where], ag_send.at[s, a], ag_recv.at[s, a], ahead)

    def ag_arrival(s, a):
        where = rows(core, at - step * s, a)
        return remote(out_ref.at[where], out_ref.at[where], ag_send.at[s, a], ag_recv.at[s, a], ahead)

    def back_copy(s, a):
        where = rows(core, at + step - step * s, a)
        return remote(out_ref.at[where], out_ref.at[where], back_send.at[s, a], back_recv.at[s, a], mate)

    def back_arrival(s, a):
        where = rows(1 - core, at - step + step * s, a)
        return remote(out_ref.at[where], out_ref.at[where], back_send.at[s, a], back_recv.at[s, a], mate)

    streams = range(STREAMS)
    for s in range(chips):
        for a in streams:
            pair_copy(s, a).start()
    for s in range(chips):
        for a in streams:
            chunk = at - step * s
            pair_arrival(s, a).wait_recv()
            total = g_ref[rows(core, chunk, a), :] + pair_buf[slot(chunk, a), :]
            if s > 0:
                rs_copy(s - 1, a).wait_recv()
                total = total + ring_buf[s - 1, a * sub : (a + 1) * sub, :]
            if s < chips - 1:
                acc[slot(chunk, a), :] = total
                rs_copy(s, a).start()
            else:
                out_ref[rows(core, chunk, a), :] = total
                ag_copy(0, a).start()
                back_copy(0, a).start()
    for s in range(chips - 1):
        for a in streams:
            ag_arrival(s, a).wait_recv()
            if s < chips - 2:
                ag_copy(s + 1, a).start()
            back_copy(s + 1, a).start()
    for s in range(chips):
        for a in streams:
            pair_copy(s, a).wait_send()
            back_copy(s, a).wait_send()
            back_arrival(s, a).wait_recv()
            if s < chips - 1:
                rs_copy(s, a).wait_send()
                ag_copy(s, a).wait_send()


def all_sum(packed, devices):
    chips = devices // 2
    rows, lanes = packed.shape
    seg = rows // devices
    vmem = pl.BlockSpec(memory_space=pltpu.VMEM)
    sems = [pltpu.SemaphoreType.DMA((chips, STREAMS)) for _ in range(8)]
    return pl.pallas_call(
        functools.partial(ring_sum, chips, seg),
        out_shape=jax.ShapeDtypeStruct(packed.shape, F32),
        in_specs=[vmem],
        out_specs=vmem,
        scratch_shapes=[
            pltpu.VMEM((chips * seg, lanes), F32),
            pltpu.VMEM((chips * seg, lanes), F32),
            pltpu.VMEM((chips - 1, seg, lanes), F32),
            *sems,
        ],
        compiler_params=pltpu.CompilerParams(
            collective_id=0, has_side_effects=True, vmem_limit_bytes=28 * 2**20
        ),
        name="ring_sum",
    )(packed)


def unpack(
    spot, cf, cc, sum_ref, out_ref, out_top, dx_ref, dx_top, *rest
):
    (coarse_out, grad_features, g1, fine_in, fine_out, g2, expand, contract, gm, merge, gc, coarse_in, coarse_proj) = rest[:13]
    sems = rest[13]
    moves = [
        (out_top, coarse_out.at[pl.ds(0, SHIFT)]),
        (out_ref.at[pl.ds(0, out_ref.shape[0] - SHIFT)], coarse_out.at[pl.ds(SHIFT, out_ref.shape[0] - SHIFT)]),
        (dx_top, grad_features.at[pl.ds(0, SHIFT)]),
        (dx_ref.at[pl.ds(0, dx_ref.shape[0] - SHIFT)], grad_features.at[pl.ds(SHIFT, dx_ref.shape[0] - SHIFT)]),
        (sum_ref.at[pl.ds(spot["merge"], 4 * cf)], merge),
        (sum_ref.at[pl.ds(spot["coarse_out"], cc)], coarse_proj),
    ]
    for name, into in (("coarse_in", coarse_in), ("expand", expand), ("contract", contract)):
        size = into.shape[0]
        for p in range(into.shape[1] // cc):
            moves.append((sum_ref.at[pl.ds(spot[name] + p * size, size)], into.at[:, pl.ds(p * cc, cc)]))
    copies = [pltpu.make_async_copy(src, dst, sems.at[i]) for i, (src, dst) in enumerate(moves)]
    for copy in copies:
        copy.start()
    top = spot["fine"]
    fine_in[:, :cc] = sum_ref[top : top + cf, :]
    fine_in[:, cc:] = sum_ref[top + cf : top + 2 * cf, :cf]
    fine_out[...] = sum_ref[top + cf : top + 2 * cf, cf:]
    g1[...] = sum_ref[top + 2 * cf : top + 2 * cf + 1, :cf]
    gains = spot["gains"]
    g2[...] = sum_ref[gains : gains + 1, :cf]
    gm[:, :cc] = sum_ref[gains + 1 : gains + 2, :]
    gm[:, cc:] = sum_ref[gains + 2 : gains + 3, :]
    gc[...] = sum_ref[gains + 3 : gains + 4, :]
    for copy in copies:
        copy.wait()


def shards(
    features,
    fine_gain_one,
    fine_project_in,
    fine_project_out,
    fine_gain_two,
    fine_expand,
    fine_contract,
    merge_gain,
    merge_weight,
    coarse_gain,
    coarse_project_in,
    coarse_project_out,
    cotangent,
):
    devices = lax.axis_size("rows")
    height, breadth, cf = features.shape
    low, narrow, cc = cotangent.shape
    units = fine_expand.shape[1]
    assert low == narrow == WIN and cc == 2 * cf and units % cc == 0
    grad_scale = 1.0 / (devices * low * narrow) ** 0.5
    win_rows, win_cols = height // WIN, breadth // WIN
    count = win_rows * win_cols
    heads = cf // HEAD_DIM
    tokens = count * TOK
    last = (lax.axis_index("rows") == devices - 1).astype(jnp.int32).reshape(1)
    vmem = pl.BlockSpec(memory_space=pltpu.VMEM)
    smem = pl.BlockSpec(memory_space=pltpu.SMEM)
    anywhere = pl.BlockSpec(memory_space=pl.ANY)

    def shape(*dims):
        return jax.ShapeDtypeStruct(dims, F32)

    def limit(mib):
        return pltpu.CompilerParams(vmem_limit_bytes=mib * 2**20)

    def shift(block, distance):
        route = [((i - distance) % devices, i) for i in range(devices)]
        return lax.ppermute(block, "rows", route)

    features_below = shift(features[:SHIFT], -1)
    cotangent_below = shift(cotangent[:SHIFT], -1)
    g1 = fine_gain_one.reshape(1, cf)
    mid, mid_head, x1, qkv, weights, ctx = pl.pallas_call(
        functools.partial(fine_forward, win_cols),
        out_shape=(
            shape(height, breadth, cf),
            shape(SHIFT, breadth, cf),
            shape(tokens, cf),
            shape(3, tokens, cf),
            shape(count, heads * TOK, TOK),
            shape(tokens, cf),
        ),
        in_specs=[smem] + [vmem] * 5,
        out_specs=(vmem,) * 6,
        scratch_shapes=[pltpu.VMEM((count, PAD, PAD, cf), F32)],
        compiler_params=limit(28),
        name="fine_forward",
    )(last, features, features_below, g1, fine_project_in, fine_project_out)
    mid_below = shift(mid_head, -1)

    spot, rows = {}, 0
    for name, size in (
        ("coarse_in", 3 * cc),
        ("coarse_out", cc),
        ("merge", 4 * cf),
        ("expand", units // cc * cf),
        ("contract", units // cc * cf),
        ("gains", 8),
        ("fine", 2 * cf + 8),
    ):
        spot[name] = rows
        rows += size
    grain = 8 * STREAMS * devices
    total_rows = -(-rows // grain) * grain
    out_slab, out_tail, dmid, dmid_tail, packed = pl.pallas_call(
        functools.partial(middle, grad_scale, spot),
        out_shape=(
            shape(low, narrow, cc),
            shape(SHIFT, narrow, cc),
            shape(height, breadth, cf),
            shape(SHIFT, breadth, cf),
            shape(total_rows, cc),
        ),
        in_specs=[smem] + [vmem] * 12,
        out_specs=(vmem,) * 5,
        scratch_shapes=[pltpu.VMEM((4 * TOK, units), F32)] * 2
        + [pltpu.VMEM((4, PAD, PAD, cf), F32), pltpu.VMEM((1, PAD, PAD, cc), F32)],
        compiler_params=limit(40),
        name="middle",
    )(
        last,
        mid,
        mid_below,
        cotangent,
        cotangent_below,
        fine_gain_two.reshape(1, cf),
        fine_expand,
        fine_contract.T,
        merge_gain.reshape(4, cf),
        merge_weight,
        coarse_gain.reshape(1, cc),
        coarse_project_in,
        coarse_project_out,
    )
    dmid_above = shift(dmid_tail, 1)
    out_above = shift(out_tail, 1)
    dx, dx_tail, packed = pl.pallas_call(
        functools.partial(fine_backward, grad_scale, spot["fine"], win_cols),
        out_shape=(
            shape(height, breadth, cf),
            shape(SHIFT, breadth, cf),
            shape(*packed.shape),
        ),
        in_specs=[vmem] * 9 + [anywhere],
        out_specs=(vmem, vmem, anywhere),
        scratch_shapes=[
            pltpu.VMEM((2 * cf + 8, cc), F32),
            pltpu.VMEM((count, PAD, PAD, cf), F32),
            pltpu.SemaphoreType.DMA(()),
        ],
        input_output_aliases={9: 2},
        compiler_params=limit(28),
        name="fine_backward",
    )(dmid, dmid_above, x1, g1, fine_project_in, fine_project_out, qkv, weights, ctx, packed)
    dx_above = shift(dx_tail, 1)
    summed = all_sum(packed, devices)
    final = pl.pallas_call(
        functools.partial(unpack, spot, cf, cc),
        out_shape=(
            shape(low, narrow, cc),
            shape(height, breadth, cf),
            shape(1, cf),
            shape(cf, 3 * cf),
            shape(cf, cf),
            shape(1, cf),
            shape(cf, units),
            shape(cf, units),
            shape(1, 4 * cf),
            shape(4 * cf, cc),
            shape(1, cc),
            shape(cc, 3 * cc),
            shape(cc, cc),
        ),
        in_specs=[vmem] * 5,
        out_specs=(anywhere, anywhere, vmem, vmem, vmem, vmem, anywhere, anywhere, vmem, anywhere, vmem, anywhere, anywhere),
        scratch_shapes=[pltpu.SemaphoreType.DMA((6 + 3 + 2 * (units // cc),))],
        compiler_params=limit(20),
        name="unpack",
    )(summed, out_slab, out_above, dx, dx_above)
    final = list(final)
    final[7] = final[7].T
    for i in (2, 5, 8, 10):
        final[i] = final[i].reshape(-1)
    return tuple(final)


def solution(mesh):
    tokens = P(("groups", "rows"), None, None)
    vector, matrix = P("groups"), P("groups", None)
    in_specs = (tokens,) + (P(),) * 11 + (tokens,)
    out_specs = (
        tokens,
        tokens,
        vector,
        matrix,
        matrix,
        vector,
        matrix,
        matrix,
        vector,
        matrix,
        vector,
        matrix,
        matrix,
    )
    return jax.shard_map(shards, mesh=mesh, in_specs=in_specs, out_specs=out_specs, check_vma=False)
```

profile of v0, /device:TPU:0, one launch (start us, length us, event | category | flops | bytes accessed | tf_op | source)
XLA Modules:
  0.0 117.1 jit_solution(8960145082297976075)
XLA Ops:
  0.6 0.8 slice.6
  1.4 5.5 %collective-permute-start = (f32[3,14,192]{2,1,0:T(8,128)S(1)}, f32[3,14,192]{2,1,0:T(8,128)S(1)}, u32[]{:S(2)}, u32[]{:S(2)}) collective-permute-start(f32[3,14,192]{2,1,0:T(8,128)S(1)} %slice.6), channel_id=1, source_target_pairs={{1,0},{2,1},{3,2},{4,3},{5,4},{6,5},{7,6},{8,7},{9,8},{10,9},{11,1... | collective-permute-start | bytes 96776 | tf_op jit(solution)/shard_map/ppermute | solution.py:528
  6.9 0.8 slice.7
  7.7 0.7 collective-permute-start.2
  8.4 0.3 collective-permute-done.halo_ref
  8.7 0.0 copy-start
  8.7 1.0 copy-done
  9.7 0.9 copy-done.4
  10.6 0.0 copy-start.9
  10.6 0.9 copy-done.9
  11.6 0.0 copy-start.11
  11.6 0.7 copy-done.11
  12.2 3.0 %fine_forward.1 = (f32[14,14,192]{2,1,0:T(8,128)S(1)}, f32[3,14,192]{2,1,0:T(8,128)S(1)}, f32[256,192]{1,0:T(8,128)S(1)}, f32[3,256,192]{2,1,0:T(8,128)S(1)}, f3...) custom-call(s32[1]{0:T(128)} %bitcast.last_ref, f32[14,14,192]{2,1,0:T(8,128)S(1)} %copy-done.9, ...), custom_call_target="tpu_custom_call" | custom-call | tf_op jit(solution)/shard_map/fine_forward/pallas_call | solution.py:533
  15.2 4.7 %collective-permute-start.1 = (f32[3,14,192]{2,1,0:T(8,128)S(1)}, f32[3,14,192]{2,1,0:T(8,128)S(1)}, u32[]{:S(2)}, u32[]{:S(2)}) collective-permute-start(f32[3,14,192]{2,1,0:T(8,128)S(1)} %get-tuple-element.41), channel_id=1, source_target_pairs={{1,0},{2,1},{3,2},{4,3},{5,4},{6,5},{7,6},{8,7},{9,8},{10,9},{11,1... | collective-permute-start | bytes 96776 | tf_op jit(solution)/shard_map/ppermute | solution.py:528
  19.9 0.7 reshape.60.gc_ref
  20.6 0.8 reshape.59.gm_ref
  21.4 0.0 collective-permute-done.2.cot_halo_ref
  21.4 0.3 collective-permute-done.1.halo_ref
  21.7 0.0 copy-start.2
  21.7 1.5 %copy-done.2 = f32[384,1152]{1,0:T(8,128)S(1)} copy-done((f32[384,1152]{1,0:T(8,128)S(1)}, f32[384,1152]{1,0:T(8,128)}, u32[]{:S(2)}) %copy-start.2) | copy-done | bytes 1769496
  23.2 0.0 copy-start.3
  23.2 1.3 %copy-done.3 = f32[768,384]{1,0:T(8,128)S(1)} copy-done((f32[768,384]{1,0:T(8,128)S(1)}, f32[768,384]{1,0:T(8,128)}, u32[]{:S(2)}) %copy-start.3) | copy-done | bytes 1179672
  24.4 0.0 copy-start.6
  24.4 1.1 copy-done.6
  25.5 0.0 copy-start.7
  25.5 1.1 copy-done.7
  26.6 0.0 copy-start.8
  26.6 1.1 copy-done.8
  27.6 0.0 copy-start.10
  27.6 0.9 copy-done.10
  28.5 0.0 copy-start.13
  28.5 0.7 copy-done.13
  29.2 0.0 copy-start.1
  29.2 11.8 %middle.1 = (f32[7,7,384]{2,1,0:T(8,128)S(1)}, f32[3,7,384]{2,1,0:T(8,128)S(1)}, f32[14,14,192]{2,1,0:T(8,128)S(1)}, f32[3,14,192]{2,1,0:T(8,128)S(1)}, f32[3584,384]{1,0:T(8,128)S(1)}) custom-call(s32[1]{0:T(128)} %bitcast.last_ref, f32[14,14,192]{2,1,0:T(8,128)S(1)} %get-tuple-element.40.mid_ref, f32[3,14,192]{2,1,0:T(8,128)S(1)} %collective-permute-done.1.halo_ref, ...), custom_call_target="tpu_custom_call" | custom-call | tf_op jit(solution)/shard_map/middle/pallas_call | solution.py:565
  41.0 0.1 collective-permute-start.3
  41.1 0.3 collective-permute-start.4
  41.4 5.9 %collective-permute-done.3.prefix_ref = f32[3,14,192]{2,1,0:T(8,128)S(1)} collective-permute-done((f32[3,14,192]{2,1,0:T(8,128)S(1)}, f32[3,14,192]{2,1,0:T(8,128)S(1)}, u32[]{:S(2)}, u32[]{:S(2)}) %collective-permute-start.3) | collective-permute-done | bytes 32288 | tf_op jit(solution)/shard_map/ppermute | solution.py:528
  47.3 0.0 copy-done.1
  47.3 0.0 copy-done.5
  47.3 0.0 copy-done.12
  47.3 4.3 %fine_backward.1 = (f32[14,14,192]{2,1,0:T(8,128)S(1)}, f32[3,14,192]{2,1,0:T(8,128)S(1)}, f32[3584,384]{1,0:T(8,128)S(1)}) custom-call(f32[14,14,192]{2,1,0:T(8,128)S(1)} %get-tuple-element.42.d_ref, f32[3,14,192]{2,1,0:T(8,128)S(1)} %collective-permute-done.3.prefix_ref, f32[256,192]{1,0:T(8,128)S(1)} %get-tuple-element.44.x_ref, ...), custom_call_target="tpu_custom_call", output_to_operand_aliasing={{2}: (9, {})} | custom-call | tf_op jit(solution)/shard_map/fine_backward/pallas_call | solution.py:597
  51.6 0.1 collective-permute-start.5
  51.7 61.0 %ring_sum.1.sum_ref = f32[3584,384]{1,0:T(8,128)S(1)} custom-call(f32[3584,384]{1,0:T(8,128)S(1)} %get-tuple-element.49.g_ref), custom_call_target="tpu_custom_call" | custom-call | tf_op jit(solution)/shard_map/ring_sum/pallas_call | solution.py:438
  112.6 0.0 collective-permute-done.4.out_top
  112.7 0.0 collective-permute-done.5.dx_top
  112.7 3.2 %unpack.1 = (f32[7,7,384]{2,1,0:T(8,128)}, f32[14,14,192]{2,1,0:T(8,128)}, f32[1,192]{1,0:T(1,128)}, f32[192,576]{1,0:T(8,128)}, f32[192,192]{1,0:T(8,128)}, /*i...) custom-call(f32[3584,384]{1,0:T(8,128)S(1)} %ring_sum.1.sum_ref, ...), custom_call_target="tpu_custom_call" | custom-call | tf_op jit(solution)/shard_map/unpack/pallas_call | solution.py:617
  115.9 0.6 reduce.1
  116.5 0.6 reduce
  (3 shorter events, 0.0 us)
Async XLA Ops:
  1.4 7.2 %collective-permute-start = (f32[3,14,192]{2,1,0:T(8,128)S(1)}, f32[3,14,192]{2,1,0:T(8,128)S(1)}, u32[]{:S(2)}, u32[]{:S(2)}) collective-permute-start(f32[3,14,192]{2,1,0:T(8,128)S(1)} %slice.6), channel_id=1, source_target_pairs={{1,0},{2,1},{3,2},{4,3},{5,4},{6,5},{7,6},{8,7},{9,8},{10,9},{11,1... | collective-permute-start | bytes 96776 | tf_op jit(solution)/shard_map/ppermute | solution.py:528
  7.7 13.7 %collective-permute-start.2 = (f32[3,7,384]{2,1,0:T(8,128)S(1)}, f32[3,7,384]{2,1,0:T(8,128)S(1)}, u32[]{:S(2)}, u32[]{:S(2)}) collective-permute-start(f32[3,7,384]{2,1,0:T(8,128)S(1)} %slice.7), channel_id=1, source_target_pairs={{1,0},{2,1},{3,2},{4,3},{5,4},{6,5},{7,6},{8,7},{9,8},{10,9},{11,1... | collective-permute-start | bytes 96776 | tf_op jit(solution)/shard_map/ppermute | solution.py:528
  8.7 1.0 copy-start
  9.7 0.9 copy-start.4
  10.6 0.9 copy-start.9
  11.6 0.7 copy-start.11
  15.2 6.4 %collective-permute-start.1 = (f32[3,14,192]{2,1,0:T(8,128)S(1)}, f32[3,14,192]{2,1,0:T(8,128)S(1)}, u32[]{:S(2)}, u32[]{:S(2)}) collective-permute-start(f32[3,14,192]{2,1,0:T(8,128)S(1)} %get-tuple-element.41), channel_id=1, source_target_pairs={{1,0},{2,1},{3,2},{4,3},{5,4},{6,5},{7,6},{8,7},{9,8},{10,9},{11,1... | collective-permute-start | bytes 96776 | tf_op jit(solution)/shard_map/ppermute | solution.py:528
  21.7 1.5 %copy-start.2 = (f32[384,1152]{1,0:T(8,128)S(1)}, f32[384,1152]{1,0:T(8,128)}, u32[]{:S(2)}) copy-start(f32[384,1152]{1,0:T(8,128)} %win_ref.4) | copy-start | bytes 5308420
  23.2 1.3 %copy-start.3 = (f32[768,384]{1,0:T(8,128)S(1)}, f32[768,384]{1,0:T(8,128)}, u32[]{:S(2)}) copy-start(f32[768,384]{1,0:T(8,128)} %wm_ref.1) | copy-start | bytes 3538948
  24.4 1.1 copy-start.6
  25.5 1.1 copy-start.7
  26.6 1.1 copy-start.8
  27.6 0.9 copy-start.10
  28.5 0.7 copy-start.13
  29.2 18.1 %copy-start.1 = (f32[192,576]{1,0:T(8,128)S(1)}, f32[192,576]{1,0:T(8,128)}, u32[]{:S(2)}) copy-start(f32[192,576]{1,0:T(8,128)} %win_ref.5) | copy-start | bytes 1327108
  29.2 18.1 %copy-start.5 = (f32[192,192]{1,0:T(8,128)S(1)}, f32[192,192]{1,0:T(8,128)}, u32[]{:S(2)}) copy-start(f32[192,192]{1,0:T(8,128)} %wout_ref.5) | copy-start | bytes 442372
  29.2 18.1 %copy-start.12 = (f32[192]{0:T(256)S(1)}, f32[192]{0:T(256)}, u32[]{:S(2)}) copy-start(f32[192]{0:T(256)} %param.14) | copy-start | bytes 2308
  41.0 6.3 %collective-permute-start.3 = (f32[3,14,192]{2,1,0:T(8,128)S(1)}, f32[3,14,192]{2,1,0:T(8,128)S(1)}, u32[]{:S(2)}, u32[]{:S(2)}) collective-permute-start(f32[3,14,192]{2,1,0:T(8,128)S(1)} %get-tuple-element.43), channel_id=1, source_target_pairs={{15,0},{0,1},{1,2},{2,3},{3,4},{4,5},{5,6},{6,7},{7,8},{8,9},{9,10... | collective-permute-start | bytes 96776 | tf_op jit(solution)/shard_map/ppermute | solution.py:528
  41.1 71.5 %collective-permute-start.4 = (f32[3,7,384]{2,1,0:T(8,128)S(1)}, f32[3,7,384]{2,1,0:T(8,128)S(1)}, u32[]{:S(2)}, u32[]{:S(2)}) collective-permute-start(f32[3,7,384]{2,1,0:T(8,128)S(1)} %get-tuple-element.51), channel_id=1, source_target_pairs={{15,0},{0,1},{1,2},{2,3},{3,4},{4,5},{5,6},{6,7},{7,8},{8,9},{9,10... | collective-permute-start | bytes 96776 | tf_op jit(solution)/shard_map/ppermute | solution.py:528
  51.6 61.0 %collective-permute-start.5 = (f32[3,14,192]{2,1,0:T(8,128)S(1)}, f32[3,14,192]{2,1,0:T(8,128)S(1)}, u32[]{:S(2)}, u32[]{:S(2)}) collective-permute-start(f32[3,14,192]{2,1,0:T(8,128)S(1)} %get-tuple-element.53), channel_id=1, source_target_pairs={{15,0},{0,1},{1,2},{2,3},{3,4},{4,5},{5,6},{6,7},{7,8},{8,9},{9,10... | collective-permute-start | bytes 96776 | tf_op jit(solution)/shard_map/ppermute | solution.py:528
where the time goes:
time: 118 us; the launch traced here: 117 us
  Pallas kernels  83.3 us (71%)
  local copies, waits for them, and re-layouts  14.1 us (12%)
  starting transfers between devices  11.2 us (9%)
  waiting for transfers between devices  6.55 us (6%)
  other arithmetic  1.2 us (1%)
    pallas_call x1, Pallas kernels, all_sum(): pl.pallas_call(functools.partial(ring_sum, chips, seg), out_shape=jax.Sha...  61 us
    pallas_call x1, Pallas kernels, shards(): pl.pallas_call(functools.partial(middle, grad_scale, spot), out_shape=(sh...  11.8 us
    ppermute x6, starting transfers between devices, shift(): return lax.ppermute(block, 'rows', route)  11.2 us
    unnamed x28, local copies, waits for them, and re-layouts  11.1 us
    ppermute x6, waiting for transfers between devices, shift(): return lax.ppermute(block, 'rows', route)  6.55 us
    pallas_call x1, Pallas kernels, shards(): pl.pallas_call(functools.partial(fine_backward, grad_scale, spot['fine'],...  4.27 us
    pallas_call x1, Pallas kernels, shards(): pl.pallas_call(functools.partial(unpack, spot, cf, cc), out_shape=(shape(...  3.24 us
    pallas_call x1, Pallas kernels, shards(): pl.pallas_call(functools.partial(fine_forward, win_cols), out_shape=(shap...  2.98 us
  transfers between devices with their start and end apart: 6, of which 3 were waited for; matrix products, arithmetic and copies ran while one was open for 2% of the time, Pallas kernels for 58%

commit v1 on v0

v1 whole, which is shorter than its diff:
```python
import functools

import jax
import jax.numpy as jnp
from jax import lax
from jax.experimental import pallas as pl
from jax.experimental.pallas import tpu as pltpu
from jax.sharding import PartitionSpec as P

HEAD_DIM = 32
WIN = 7
PAD = 8
TOK = PAD * PAD
SHIFT = 3
EPSILON = 1e-05
MESH = pl.DeviceIdType.MESH
F32 = jnp.float32
BF16 = jnp.bfloat16
NN = (((1,), (0,)), ((), ()))
NT = (((1,), (1,)), ((), ()))
TN = (((0,), (0,)), ((), ()))


def halves(a):
    hi = a.astype(BF16)
    return hi, (a - hi.astype(F32)).astype(BF16)


def mm(a, b, dims=NN):
    a = a if isinstance(a, tuple) else halves(a)
    b = b if isinstance(b, tuple) else halves(b)
    dot = functools.partial(lax.dot_general, dimension_numbers=dims, preferred_element_type=F32)
    return dot(a[0], b[0]) + (dot(a[0], b[1]) + dot(a[1], b[0]))


def runs(first, count, breadth):
    head = min(count, breadth - first % breadth)
    pieces = [(0, first % breadth, head)]
    return pieces + ([(head, 0, count - head)] if head < count else [])


def fill_windows(dst, row_of, win_row, win_cols, breadth):
    for col in range(win_cols):
        for i in range(WIN):
            ref, at = row_of(win_row * WIN + i)
            for place, start, size in runs(col * WIN + SHIFT, WIN, breadth):
                dst[win_row * win_cols + col, i, place : place + size, :] = ref[at, start : start + size, :]


def put_windows(dst, top, src, win_row, win_cols):
    breadth = dst.shape[1]
    for col in range(win_cols):
        for place, start, size in runs(col * WIN + SHIFT, WIN, breadth):
            dst[top : top + WIN, start : start + size, :] = src[
                win_row * win_cols + col, :WIN, place : place + size, :
            ]


def norm(v):
    centered = v - jnp.mean(v, axis=-1, keepdims=True)
    scale = lax.rsqrt(jnp.mean(centered * centered, axis=-1, keepdims=True) + EPSILON)
    return centered * scale, scale


def norm_back(dn, n, scale):
    return scale * (
        dn - jnp.mean(dn, axis=-1, keepdims=True) - n * jnp.mean(dn * n, axis=-1, keepdims=True)
    )


def spread(a, heads):
    lane = lax.broadcasted_iota(jnp.int32, a.shape, 1) // HEAD_DIM
    return jnp.concatenate([jnp.where(lane == h, a, 0.0) for h in range(heads)], axis=0)


def gather_heads(a, heads):
    rows = a.shape[0] // heads
    lane = lax.broadcasted_iota(jnp.int32, (rows, a.shape[1]), 1) // HEAD_DIM
    total = jnp.where(lane == 0, a[:rows], 0.0)
    for h in range(1, heads):
        total = jnp.where(lane == h, a[h * rows : (h + 1) * rows], total)
    return total


def allowed(last_row, last_col):
    def label(axis):
        t = lax.broadcasted_iota(jnp.int32, (TOK, TOK), axis)
        r, c = t // PAD, t % PAD
        lab = jnp.where(r >= WIN - SHIFT, last_row * 2, 0) + jnp.where(
            c >= WIN - SHIFT, last_col, 0
        )
        return lab, (r < WIN) & (c < WIN)

    lq, _ = label(0)
    lk, real = label(1)
    return (lq == lk) & real


def attend(q, k, v, mask, heads):
    s = mm(spread(q, heads), k, NT) * HEAD_DIM**-0.5
    s = jnp.where(jnp.concatenate([mask] * heads, axis=0), s, -1e30)
    w = jnp.exp(s - jnp.max(s, axis=-1, keepdims=True))
    w = w / jnp.sum(w, axis=-1, keepdims=True)
    return w, gather_heads(mm(w, v), heads)


def attend_back(dctx, q, k, v, w, heads):
    dc = halves(spread(dctx, heads))
    dw = mm(dc, v, NT)
    dv = mm(w, dc, TN)
    ds = w * (dw - jnp.sum(dw * w, axis=-1, keepdims=True)) * HEAD_DIM**-0.5
    ds = halves(ds)
    dq = gather_heads(mm(ds, k), heads)
    dk = mm(ds, spread(q, heads), TN)
    return dq, dk, dv


LOADS = ("features", "fine_in", "fine_out", "cotangent", "expand", "contract", "merge", "coarse_in", "coarse_out")


class Ring:
    def __init__(self, chips, rounds, g, out, pair_buf, acc, ring_buf, sems):
        self.chips, self.rounds = chips, rounds
        self.g, self.out, self.pair_buf, self.acc, self.ring_buf = g, out, pair_buf, acc, ring_buf
        (self.pair_send, self.pair_recv, self.rs_send, self.rs_recv, self.ag_send, self.ag_recv, self.back_send, self.back_recv) = sems
        me = lax.axis_index("rows")
        self.core, chip = me % 2, me // 2
        column, line = chip % 2, chip // 2
        self.at = jnp.where(column == 0, line, chips - 1 - line)
        self.step = 1 - 2 * self.core
        self.ahead, self.behind = self.device(self.at + self.step), self.device(self.at - self.step)
        self.mate = me + 1 - 2 * self.core

    def device(self, q):
        chips = self.chips
        q = (q + chips) % chips
        return jnp.where(q < chips // 2, q * 2, (chips - 1 - q) * 2 + 1) * 2 + self.core

    def slot(self, r, chunk):
        top, seg = self.rounds[r]
        chunk = (chunk + 2 * self.chips) % self.chips
        return pl.ds(pl.multiple_of(top // 2 + chunk * seg, 8), seg)

    def rows(self, r, half, chunk):
        top, seg = self.rounds[r]
        chunk = (chunk + 2 * self.chips) % self.chips
        return pl.ds(pl.multiple_of(top + (half * self.chips + chunk) * seg, 8), seg)

    def landing(self, r, s):
        top, seg = self.rounds[r]
        return pl.ds(top // 2 + s * seg, seg)

    def remote(self, src, dst, send, recv, target):
        return pltpu.make_async_remote_copy(
            src_ref=src, dst_ref=dst, send_sem=send, recv_sem=recv, device_id={"rows": target}, device_id_type=MESH
        )

    def pair_copy(self, r, s, sign=1):
        chunk = self.at + sign * self.step * s
        return self.remote(
            self.g.at[self.rows(r, 1 - self.core, chunk)],
            self.pair_buf.at[self.slot(r, chunk)],
            self.pair_send.at[r, s],
            self.pair_recv.at[r, s],
            self.mate,
        )

    def rs_copy(self, r, s):
        return self.remote(
            self.acc.at[self.slot(r, self.at - self.step * s)],
            self.ring_buf.at[self.landing(r, s)],
            self.rs_send.at[r, s],
            self.rs_recv.at[r, s],
            self.ahead,
        )

    def ag_copy(self, r, s, shift):
        where = self.rows(r, self.core, self.at + shift * self.step - self.step * s)
        return self.remote(self.out.at[where], self.out.at[where], self.ag_send.at[r, s], self.ag_recv.at[r, s], self.ahead)

    def back_copy(self, r, s):
        where = self.rows(r, self.core, self.at + self.step - self.step * s)
        return self.remote(self.out.at[where], self.out.at[where], self.back_send.at[r, s], self.back_recv.at[r, s], self.mate)

    def back_arrival(self, r, s):
        where = self.rows(r, 1 - self.core, self.at - self.step + self.step * s)
        return self.remote(self.out.at[where], self.out.at[where], self.back_send.at[r, s], self.back_recv.at[r, s], self.mate)

    def launch(self, r):
        for s in range(self.chips):
            self.pair_copy(r, s).start()

    def advance(self, r, s):
        chips = self.chips
        if s < chips:
            chunk = self.at - self.step * s
            self.pair_copy(r, s, -1).wait_recv()
            total = self.g[self.rows(r, self.core, chunk), :] + self.pair_buf[self.slot(r, chunk), :]
            if s > 0:
                self.rs_copy(r, s - 1).wait_recv()
                total = total + self.ring_buf[self.landing(r, s - 1), :]
            if s < chips - 1:
                self.acc[self.slot(r, chunk), :] = total
                self.rs_copy(r, s).start()
            else:
                self.out[self.rows(r, self.core, chunk), :] = total
                self.ag_copy(r, 0, 1).start()
                self.back_copy(r, 0).start()
        else:
            s -= chips
            self.ag_copy(r, s, 0).wait_recv()
            if s < chips - 2:
                self.ag_copy(r, s + 1, 1).start()
            self.back_copy(r, s + 1).start()

    def finish(self, r):
        for s in range(self.chips):
            self.pair_copy(r, s).wait_send()
            self.back_copy(r, s).wait_send()
            self.back_arrival(r, s).wait_recv()
            if s < self.chips - 1:
                self.rs_copy(r, s).wait_send()
                self.ag_copy(r, s, 1).wait_send()


def whole_step(
    grad_scale, chips, spot, rounds, win_cols,
    features, fine_in, fine_out, cotangent, expand, contract, merge, coarse_in, coarse_out,
    g1_ref, g2_ref, gm_ref, gc_ref,
    out_ref, dx_ref, sum_ref,
    f_ref, fin, fout, cot_ref, we, wc, wm, cin, cout,
    f_halo, cot_halo, mid_halo, prefix,
    cells, x_ref, qkv_ref, w_ref, ctx_ref, dqkv_ref, d_all,
    mid_ref, dmid_ref, out_frame, dx_frame, coarse_cells, quads, h_ref, act_ref,
    pack_ref, pair_buf, acc, ring_buf,
    load_sem, halo_send, halo_recv, local_sem, *ring_sems,
):
    height, breadth, cf = f_ref.shape
    cc = cot_ref.shape[2]
    low = cot_ref.shape[0]
    heads, coarse_heads = cf // HEAD_DIM, cc // HEAD_DIM
    win_rows = height // WIN
    n = 2 * chips
    me = lax.axis_index("rows")
    above, below = (me + n - 1) % n, (me + 1) % n
    last = (me == n - 1).astype(jnp.int32)

    sources = (features, fine_in, fine_out, cotangent, expand, contract, merge, coarse_in, coarse_out)
    targets = (f_ref, fin, fout, cot_ref, we, wc, wm, cin, cout)
    loads = {
        name: pltpu.make_async_copy(src, dst, load_sem.at[i])
        for i, (name, src, dst) in enumerate(zip(LOADS, sources, targets))
    }
    for name in LOADS:
        loads[name].start()

    ring = Ring(chips, rounds, pack_ref, sum_ref, pair_buf, acc, ring_buf, ring_sems)
    barrier = pltpu.get_barrier_semaphore()
    for other in (above, below, ring.ahead, ring.behind, ring.mate):
        pl.semaphore_signal(barrier, inc=1, device_id={"rows": other}, device_id_type=MESH)
    pl.semaphore_wait(barrier, 5)

    def halo(i, src, dst, target):
        return ring.remote(src, dst, halo_send.at[i], halo_recv.at[i], target)

    send_f = halo(0, features.at[pl.ds(0, SHIFT)], f_halo, above)
    send_cot = halo(1, cotangent.at[pl.ds(0, SHIFT)], cot_halo, above)
    send_mid = halo(2, mid_ref.at[pl.ds(0, SHIFT)], mid_halo, above)
    send_out = halo(3, out_frame.at[pl.ds(low - SHIFT, SHIFT)], out_ref.at[pl.ds(0, SHIFT)], below)
    send_dmid = halo(4, dmid_ref.at[pl.ds(height - SHIFT, SHIFT)], prefix, below)
    send_dx = halo(5, dx_frame.at[pl.ds(height - SHIFT, SHIFT)], dx_ref.at[pl.ds(0, SHIFT)], below)
    send_f.start()
    send_cot.start()

    cells[...] = jnp.zeros_like(cells)
    quads[...] = jnp.zeros_like(quads)
    g1 = g1_ref[...].reshape(1, cf)
    rows_per = win_cols * TOK

    def window_mask(win_row, col):
        return allowed(last if win_row == win_rows - 1 else 0, int(col == win_cols - 1))

    loads["features"].wait()
    for wr in range(win_rows):
        if wr == win_rows - 1:
            send_f.wait_recv()
        fill_windows(
            cells,
            lambda r: (f_ref, r + SHIFT) if r + SHIFT < height else (f_halo, r + SHIFT - height),
            wr, win_cols, breadth,
        )
        at = slice(wr * rows_per, (wr + 1) * rows_per)
        x = cells[wr * win_cols : (wr + 1) * win_cols].reshape(rows_per, cf)
        x_ref[at, :] = x
        unit, _ = norm(x)
        u = halves(unit * g1)
        if wr == 0:
            loads["fine_in"].wait()
        parts = []
        for part in range(3):
            got = mm(u, fin[:, part * cf : (part + 1) * cf])
            qkv_ref[part, at, :] = got
            parts.append(got)
        for col in range(win_cols):
            i = wr * win_cols + col
            inside = slice(col * TOK, (col + 1) * TOK)
            w, ctx = attend(parts[0][inside], parts[1][inside], parts[2][inside], window_mask(wr, col), heads)
            w_ref[i] = w
            ctx_ref[i * TOK : (i + 1) * TOK, :] = ctx
        if wr == 0:
            loads["fine_out"].wait()
        mid = x + mm(ctx_ref[at, :], fout[...])
        cells[wr * win_cols : (wr + 1) * win_cols] = mid.reshape(win_cols, PAD, PAD, cf)
        put_windows(mid_ref, wr * WIN, cells, wr, win_cols)
        if wr == 0:
            send_mid.start()

    g2 = g2_ref[...].reshape(1, cf)
    gmv = gm_ref[...].reshape(1, 4 * cf)
    gm = [gmv[:, k * cf : (k + 1) * cf] for k in range(4)]
    gc = gc_ref[...].reshape(1, cc)
    send_mid.wait_recv()
    for k in range(4):
        dj, di = divmod(k, 2)
        for i in range(WIN):
            r = SHIFT + 2 * i + di
            ref, r = (mid_ref, r) if r < height else (mid_halo, r - height)
            for j in range(WIN):
                at = (2 * (SHIFT + j) + dj) % breadth
                quads[k, i, j : j + 1, :] = ref[r, at : at + 1, :]
    x = quads[...].reshape(4 * TOK, cf)
    n2, r2 = norm(x)
    u2 = halves(n2 * g2)
    loads["expand"].wait()
    h = mm(u2, we[...])
    h_ref[...] = h
    act = h * (0.5 * (1.0 + lax.erf(h * 0.5**0.5)))
    act_ref[...] = act
    loads["contract"].wait()
    y = x + mm(act, wc[...], NT)
    ys = [y[k * TOK : (k + 1) * TOK] for k in range(4)]
    wide = 1.0 / (4 * cf)
    mean = sum(jnp.sum(v, axis=-1, keepdims=True) for v in ys) * wide
    ys = [v - mean for v in ys]
    rm = lax.rsqrt(sum(jnp.sum(v * v, axis=-1, keepdims=True) for v in ys) * wide + EPSILON)
    nm = [v * rm for v in ys]
    um = [halves(nm[k] * gm[k]) for k in range(4)]
    loads["merge"].wait()
    merged = sum(mm(um[k], wm[k * cf : (k + 1) * cf, :]) for k in range(4))
    nc, rc = norm(merged)
    uc = halves(nc * gc)
    loads["coarse_in"].wait()
    q, k_, v_ = (mm(uc, cin[:, p * cc : (p + 1) * cc]) for p in range(3))
    w, ctx = attend(q, k_, v_, allowed(last, 1), coarse_heads)
    loads["coarse_out"].wait()
    coarse_cells[0] = (merged + mm(ctx, cout[...])).reshape(PAD, PAD, cc)
    put_windows(out_frame, 0, coarse_cells, 0, 1)
    send_out.start()

    loads["cotangent"].wait()
    send_cot.wait_recv()
    coarse_cells[...] = jnp.zeros_like(coarse_cells)
    fill_windows(
        coarse_cells,
        lambda r: (cot_ref, r + SHIFT) if r + SHIFT < low else (cot_halo, r + SHIFT - low),
        0, 1, low,
    )
    cot = coarse_cells[0].reshape(TOK, cc)
    ch = halves(cot)
    pack_ref[spot["coarse_out"] : spot["coarse_out"] + cc, :] = mm(ctx, ch, TN) * grad_scale
    dctx = mm(ch, cout[...], NT)
    got = attend_back(dctx, q, k_, v_, w, coarse_heads)
    du = 0.0
    for p in range(3):
        dp = halves(got[p])
        top = spot["coarse_in", p]
        pack_ref[top : top + cc, :] = mm(uc, dp, TN) * grad_scale
        du += mm(dp, cin[:, p * cc : (p + 1) * cc], NT)
        if p == 0:
            ring.launch(0)
    ring.launch(1)
    ring.advance(0, 0)
    gains = spot["gains"]
    pack_ref[gains:, :] = jnp.zeros_like(pack_ref[gains:, :])
    pack_ref[gains + 3 : gains + 4, :] = jnp.sum(du * nc, axis=0, keepdims=True) * grad_scale
    dm = cot + norm_back(du * gc, nc, rc)
    mh = halves(dm)
    dn = []
    for k in range(4):
        top = spot["merge"] + k * cf
        pack_ref[top : top + cf, :] = mm(um[k], mh, TN) * grad_scale
        dk = mm(mh, wm[k * cf : (k + 1) * cf, :], NT)
        row = gains + 1 + k // 2
        pack_ref[row : row + 1, (k % 2) * cf : (k % 2 + 1) * cf] = jnp.sum(dk * nm[k], axis=0, keepdims=True) * grad_scale
        dn.append(dk * gm[k])
    ring.launch(2)
    ring.advance(1, 0)
    ring.advance(0, 1)
    m1 = sum(jnp.sum(v, axis=-1, keepdims=True) for v in dn) * wide
    m2 = sum(jnp.sum(dn[k] * nm[k], axis=-1, keepdims=True) for k in range(4)) * wide
    dy = jnp.concatenate([rm * (dn[k] - m1 - nm[k] * m2) for k in range(4)], axis=0)
    yh = halves(dy)
    dwc = mm(yh, act_ref[...], TN) * grad_scale
    top = spot["contract"]
    for p in range(dwc.shape[1] // cc):
        pack_ref[top + p * cf : top + (p + 1) * cf, :] = dwc[:, p * cc : (p + 1) * cc]
    ring.advance(2, 0)
    ring.advance(1, 1)
    ring.advance(0, 2)
    h = h_ref[...]
    slope = 0.5 * (1.0 + lax.erf(h * 0.5**0.5)) + h * (jnp.exp(-0.5 * h * h) * 0.3989422804014327)
    dh = halves(mm(yh, wc[...]) * slope)
    dwe = mm(u2, dh, TN) * grad_scale
    top = spot["expand"]
    for p in range(dwe.shape[1] // cc):
        pack_ref[top + p * cf : top + (p + 1) * cf, :] = dwe[:, p * cc : (p + 1) * cc]
    ring.launch(3)
    du2 = mm(dh, we[...], NT)
    pack_ref[gains : gains + 1, :cf] = jnp.sum(du2 * n2, axis=0, keepdims=True) * grad_scale
    quads[...] = (dy + norm_back(du2 * g2, n2, r2)).reshape(quads.shape)
    for k in range(4):
        dj, di = divmod(k, 2)
        for i in range(WIN):
            for j in range(WIN):
                at = (2 * (SHIFT + j) + dj) % breadth
                dmid_ref[2 * i + di, at : at + 1, :] = quads[k, i, j : j + 1, :]
    send_dmid.start()
    ring.advance(3, 0)
    ring.advance(2, 1)
    ring.advance(1, 2)
    ring.advance(0, 3)

    for w0 in range(cells.shape[0]):
        cells[w0, WIN:, :, :] = jnp.zeros_like(cells[w0, WIN:, :, :])
        cells[w0, :, WIN:, :] = jnp.zeros_like(cells[w0, :, WIN:, :])
    for wr in reversed(range(win_rows)):
        if wr == 0:
            send_dmid.wait_recv()
        fill_windows(
            cells, lambda r: (dmid_ref, r - SHIFT) if r >= SHIFT else (prefix, r), wr, win_cols, breadth
        )
        at = slice(wr * rows_per, (wr + 1) * rows_per)
        d = cells[wr * win_cols : (wr + 1) * win_cols].reshape(rows_per, cf)
        d_all[at, :] = d
        unit, scale = norm(x_ref[at, :])
        dctx = mm(d, fout[...], NT)
        for col in range(win_cols):
            i = wr * win_cols + col
            inside = slice(i * TOK, (i + 1) * TOK)
            got = attend_back(
                dctx[col * TOK : (col + 1) * TOK], qkv_ref[0, inside, :], qkv_ref[1, inside, :], qkv_ref[2, inside, :], w_ref[i], heads
            )
            for part in range(3):
                dqkv_ref[part, inside, :] = got[part]
        du = 0.0
        for part in range(3):
            du += mm(dqkv_ref[part, at, :], fin[:, part * cf : (part + 1) * cf], NT)
        gain_part = jnp.sum(du * unit, axis=0, keepdims=True)
        gain_one = gain_part if wr == win_rows - 1 else gain_one + gain_part
        cells[wr * win_cols : (wr + 1) * win_cols] = (d + norm_back(du * g1, unit, scale)).reshape(win_cols, PAD, PAD, cf)
        put_windows(dx_frame, wr * WIN, cells, wr, win_cols)
        if wr == win_rows - 1:
            send_dx.start()
        shift = win_rows - 1 - wr
        for r in range(4):
            ring.advance(3 - r, 1 + shift + r)
    unit, _ = norm(x_ref[...])
    u = halves(unit * g1)
    weight = [mm(u, dqkv_ref[part], TN) * grad_scale for part in range(3)]
    dwout = mm(ctx_ref[...], d_all[...], TN) * grad_scale
    top = spot["fine"]
    pack_ref[top : top + cf, :] = jnp.concatenate(weight[:2], axis=1)
    pack_ref[top + cf : top + 2 * cf, :] = jnp.concatenate([weight[2], dwout], axis=1)
    pack_ref[gains + 4 : gains + 5, :cf] = gain_one * grad_scale
    ring.launch(4)

    keep_out = pltpu.make_async_copy(
        out_frame.at[pl.ds(0, low - SHIFT)], out_ref.at[pl.ds(SHIFT, low - SHIFT)], local_sem.at[0]
    )
    keep_dx = pltpu.make_async_copy(
        dx_frame.at[pl.ds(0, height - SHIFT)], dx_ref.at[pl.ds(SHIFT, height - SHIFT)], local_sem.at[1]
    )
    keep_out.start()
    keep_dx.start()
    count = len(rounds)
    starts = [0, 1, 2, 3, 5]
    done = [1 + win_rows + 3 - r for r in range(4)] + [0]
    steps = 2 * chips - 1
    todo = sorted(
        (s + starts[r], r, s) for r in range(count) for s in range(done[r], steps)
    )
    for _, r, s in todo:
        ring.advance(r, s)
    for r in range(count):
        ring.finish(r)
    keep_out.wait()
    keep_dx.wait()
    for copy in (send_f, send_cot, send_mid, send_out, send_dmid, send_dx):
        copy.wait_send()
    send_out.wait_recv()
    send_dx.wait_recv()


def unpack(spot, cf, cc, sum_ref, out_ref, dx_ref, *rest):
    (coarse_out, grad_features, g1, fine_in, fine_out, g2, expand, contract, gm, merge, gc, coarse_in, coarse_proj) = rest[:13]
    sems = rest[13]
    moves = [
        (out_ref, coarse_out),
        (dx_ref, grad_features),
        (sum_ref.at[pl.ds(spot["merge"], 4 * cf)], merge),
        (sum_ref.at[pl.ds(spot["coarse_out"], cc)], coarse_proj),
    ]
    for name, into in (("coarse_in", coarse_in), ("expand", expand), ("contract", contract)):
        size = into.shape[0]
        for p in range(into.shape[1] // cc):
            at = spot[name, p] if (name, p) in spot else spot[name] + p * size
            moves.append((sum_ref.at[pl.ds(at, size)], into.at[:, pl.ds(p * cc, cc)]))
    copies = [pltpu.make_async_copy(src, dst, sems.at[i]) for i, (src, dst) in enumerate(moves)]
    for copy in copies:
        copy.start()
    top = spot["fine"]
    fine_in[:, :cc] = sum_ref[top : top + cf, :]
    fine_in[:, cc:] = sum_ref[top + cf : top + 2 * cf, :cf]
    fine_out[...] = sum_ref[top + cf : top + 2 * cf, cf:]
    gains = spot["gains"]
    g1[...] = sum_ref[gains + 4 : gains + 5, :cf].reshape(g1.shape)
    g2[...] = sum_ref[gains : gains + 1, :cf].reshape(g2.shape)
    gm[...] = jnp.concatenate([sum_ref[gains + 1 : gains + 2, :], sum_ref[gains + 2 : gains + 3, :]], axis=1).reshape(gm.shape)
    gc[...] = sum_ref[gains + 3 : gains + 4, :].reshape(gc.shape)
    for copy in copies:
        copy.wait()


def shards(
    features,
    fine_gain_one,
    fine_project_in,
    fine_project_out,
    fine_gain_two,
    fine_expand,
    fine_contract,
    merge_gain,
    merge_weight,
    coarse_gain,
    coarse_project_in,
    coarse_project_out,
    cotangent,
):
    devices = lax.axis_size("rows")
    chips = devices // 2
    height, breadth, cf = features.shape
    low, narrow, cc = cotangent.shape
    units = fine_expand.shape[1]
    assert low == narrow == WIN and cc == 2 * cf and units % cc == 0
    grad_scale = 1.0 / (devices * low * narrow) ** 0.5
    win_rows, win_cols = height // WIN, breadth // WIN
    count = win_rows * win_cols
    heads = cf // HEAD_DIM
    tokens = count * TOK
    vmem = pl.BlockSpec(memory_space=pltpu.VMEM)
    anywhere = pl.BlockSpec(memory_space=pl.ANY)

    def shape(*dims):
        return jax.ShapeDtypeStruct(dims, F32)

    def limit(mib):
        return pltpu.CompilerParams(vmem_limit_bytes=mib * 2**20)

    grain = 8 * devices
    spot, rounds, rows = {}, [], 0
    strips = units // cc * cf
    plan = (
        (("coarse_out", cc), (("coarse_in", 0), cc)),
        ((("coarse_in", 1), cc), (("coarse_in", 2), cc)),
        (("merge", 4 * cf),),
        (("contract", strips), ("expand", strips)),
        (("fine", 2 * cf), ("gains", 8)),
    )
    for group in plan:
        top = rows
        for name, size in group:
            spot[name] = rows
            rows += size
        padded = -(-(rows - top) // grain) * grain
        rounds.append((top, padded // devices))
        rows = top + padded
    total = rows
    scratch = [
        pltpu.VMEM(a.shape, F32)
        for a in (
            features, fine_project_in, fine_project_out, cotangent, fine_expand, fine_expand, merge_weight, coarse_project_in, coarse_project_out,
        )
    ]
    scratch += [
        pltpu.VMEM(dims, F32)
        for dims in (
            (SHIFT, breadth, cf),
            (SHIFT, narrow, cc),
            (SHIFT, breadth, cf),
            (SHIFT, breadth, cf),
            (count, PAD, PAD, cf),
            (tokens, cf),
            (3, tokens, cf),
            (count, heads * TOK, TOK),
            (tokens, cf),
            (3, tokens, cf),
            (tokens, cf),
            (height, breadth, cf),
            (height, breadth, cf),
            (low, narrow, cc),
            (height, breadth, cf),
            (1, PAD, PAD, cc),
            (4, PAD, PAD, cf),
            (4 * TOK, units),
            (4 * TOK, units),
            (total, cc),
            (total // 2, cc),
            (total // 2, cc),
            (total // 2, cc),
        )
    ]
    dma = pltpu.SemaphoreType.DMA
    scratch += [dma((len(LOADS),)), dma((6,)), dma((6,)), dma((2,))]
    scratch += [dma((len(rounds), chips)) for _ in range(8)]
    out_slab, dx, summed = pl.pallas_call(
        functools.partial(whole_step, grad_scale, chips, spot, rounds, win_cols),
        out_shape=(shape(low, narrow, cc), shape(height, breadth, cf), shape(total, cc)),
        in_specs=[anywhere] * 9 + [vmem] * 4,
        out_specs=(vmem,) * 3,
        scratch_shapes=scratch,
        compiler_params=pltpu.CompilerParams(
            collective_id=0, has_side_effects=True, vmem_limit_bytes=50 * 2**20
        ),
        name="whole_step",
    )(
        features, fine_project_in, fine_project_out, cotangent, fine_expand, fine_contract.T, merge_weight, coarse_project_in, coarse_project_out,
        fine_gain_one, fine_gain_two, merge_gain, coarse_gain,
    )
    final = pl.pallas_call(
        functools.partial(unpack, spot, cf, cc),
        out_shape=(
            shape(low, narrow, cc),
            shape(height, breadth, cf),
            shape(cf),
            shape(cf, 3 * cf),
            shape(cf, cf),
            shape(cf),
            shape(cf, units),
            shape(cf, units),
            shape(4 * cf),
            shape(4 * cf, cc),
            shape(cc),
            shape(cc, 3 * cc),
            shape(cc, cc),
        ),
        in_specs=[vmem] * 3,
        out_specs=(anywhere, anywhere, vmem, vmem, vmem, vmem, anywhere, anywhere, vmem, anywhere, vmem, anywhere, anywhere),
        scratch_shapes=[pltpu.SemaphoreType.DMA((4 + 3 + 2 * (units // cc),))],
        compiler_params=limit(20),
        name="unpack",
    )(summed, out_slab, dx)
    final = list(final)
    final[7] = final[7].T
    return tuple(final)


def solution(mesh):
    tokens = P(("groups", "rows"), None, None)
    vector, matrix = P("groups"), P("groups", None)
    in_specs = (tokens,) + (P(),) * 11 + (tokens,)
    out_specs = (
        tokens,
        tokens,
        vector,
        matrix,
        matrix,
        vector,
        matrix,
        matrix,
        vector,
        matrix,
        vector,
        matrix,
        matrix,
    )
    return jax.shard_map(shards, mesh=mesh, in_specs=in_specs, out_specs=out_specs, check_vma=False)
```

time: 118 us -> 117 us (level)
  Pallas kernels: 83.3 us -> 103 us
  starting transfers between devices: 11.2 us -> 0 us
  waiting for transfers between devices: 6.55 us -> 0 us
  local copies, waits for them, and re-layouts: 14.1 us -> 12.2 us
  other arithmetic: 1.2 us -> 0 us
    pallas_call x4 -> x1, Pallas kernels: 80 us -> 99.7 us  [shards(): pl.pallas_call(functools.partial(whole_step, grad_scale, chips, spot, rou...]
    ppermute x6 -> x0, starting transfers between devices: 11.2 us -> none  [shift(): return lax.ppermute(block, 'rows', route)]
    ppermute x6 -> x0, waiting for transfers between devices: 6.55 us -> none  [shift(): return lax.ppermute(block, 'rows', route)]
    slice x2 -> x0, local copies, waits for them, and re-layouts: 1.58 us -> none  [the longest x1 0.8 us: shards(): features_below = shift(features[:SHIFT], -1)]
    reshape x2 -> x0, local copies, waits for them, and re-layouts: 1.45 us -> none  [the longest x1 0.76 us: shards(): merge_gain.reshape(4, cf)]
    pallas_call x2 -> x0, other arithmetic: 1.2 us -> none  [shards(): pl.pallas_call(functools.partial(unpack, spot, cf, cc), out_shape=(shape(...]
    unnamed x28 -> x24, local copies, waits for them, and re-layouts: 11.1 us -> 12.2 us
  transfers between devices with their start and end apart: 6 -> 0, of which waited for: 3 -> 0; matrix products, arithmetic and copies ran while one was open for 2% -> 0% of each run, Pallas kernels for 58% -> 0%
where the time goes in v1:
time: 117 us; the launch traced here: 116 us
  Pallas kernels  103 us (88%)
  local copies, waits for them, and re-layouts  12.2 us (10%)
    pallas_call x1, Pallas kernels, shards(): pl.pallas_call(functools.partial(whole_step, grad_scale, chips, spot, rou...  99.7 us
    unnamed x24, local copies, waits for them, and re-layouts  12.2 us
    pallas_call x1, Pallas kernels, shards(): pl.pallas_call(functools.partial(unpack, spot, cf, cc), out_shape=(shape(...  3.22 us

profile of v1, /device:TPU:0, one launch (start us, length us, event | category | flops | bytes accessed | tf_op | source)
XLA Modules:
  0.0 116.0 jit_solution(14270141396927298544)
XLA Ops:
  0.6 0.0 copy-start.1
  0.7 1.1 copy-done.1
  1.7 0.0 copy-start.2
  1.7 1.1 copy-done.2
  2.8 0.0 copy-start.3
  2.8 1.1 copy-done.3
  3.8 0.0 copy-start.4
  3.8 1.0 copy-done.4
  4.9 0.0 copy-start.5
  4.9 0.9 copy-done.5
  5.8 0.0 copy-start.6
  5.8 0.9 copy-done.6
  6.7 0.0 copy-start.7
  6.7 0.9 copy-done.7
  7.6 0.0 copy-start.8
  7.6 0.7 copy-done.8
  8.3 0.0 copy-start.9
  8.3 0.7 copy-done.9
  9.0 0.0 copy-start.10
  9.0 0.7 copy-done.10
  9.7 0.0 copy-start.11
  9.7 0.7 copy-done.11
  10.4 99.7 %whole_step.1 = (f32[7,7,384]{2,1,0:T(8,128)S(1)}, f32[14,14,192]{2,1,0:T(8,128)S(1)}, f32[3584,384]{1,0:T(8,128)}) custom-call(f32[14,14,192]{2,1,0:T(8,128)S(1)} %copy-done.5, f32[192,576]{1,0:T(8,128)S(1)} %copy-done.4, f32[192,192]{1,0:T(8,128)S(1)} %copy-done.6, f32[7,7,384]{2,1,0:T(8,128)S(1)} %copy-done.7, f32[192,768]{1,0:T(8,128)S(1)} %copy-done.1, ...), custom_call_target="tpu_custom_call" | custom-call | tf_op jit(solution)/shard_map/whole_step/pallas_call | solution.py:625
  110.1 0.0 copy-start
  110.1 2.6 %copy-done = f32[3584,384]{1,0:T(8,128)S(1)} copy-done((f32[3584,384]{1,0:T(8,128)S(1)}, f32[3584,384]{1,0:T(8,128)}, u32[]{:S(2)}) %copy-start) | copy-done | bytes 5505048
  112.7 3.2 %unpack.1 = (f32[7,7,384]{2,1,0:T(8,128)}, f32[14,14,192]{2,1,0:T(8,128)}, f32[192]{0:T(256)}, f32[192,576]{1,0:T(8,128)}, f32[192,192]{1,0:T(8,128)}, /*index=5...) custom-call(f32[3584,384]{1,0:T(8,128)S(1)} %copy-done, ...), custom_call_target="tpu_custom_call" | custom-call | tf_op jit(solution)/shard_map/unpack/pallas_call | solution.py:639
Async XLA Ops:
  0.6 1.1 copy-start.1
  1.7 1.1 copy-start.2
  2.8 1.1 copy-start.3
  3.8 1.0 copy-start.4
  4.9 0.9 copy-start.5
  5.8 0.9 copy-start.6
  6.7 0.9 copy-start.7
  7.6 0.7 copy-start.8
  8.3 0.7 copy-start.9
  9.0 0.7 copy-start.10
  9.7 0.7 copy-start.11
  110.1 2.6 %copy-start = (f32[3584,384]{1,0:T(8,128)S(1)}, f32[3584,384]{1,0:T(8,128)}, u32[]{:S(2)}) copy-start(f32[3584,384]{1,0:T(8,128)} %get-tuple-element.29.sum_ref) | copy-start | bytes 16515076

commit v2 on v1

--- a/solution.py
+++ b/solution.py
@@ -115,7 +115,9 @@
     return dq, dk, dv
 
 
-LOADS = ("features", "fine_in", "fine_out", "cotangent", "expand", "contract", "merge", "coarse_in", "coarse_out")
+LOADS = (
+    "features", "g1", "fine_in", "fine_out", "g2", "expand", "contract", "gm", "merge", "gc", "coarse_in", "coarse_out", "cotangent",
+)
 
 
 class Ring:
@@ -225,10 +227,9 @@
 
 def whole_step(
     grad_scale, chips, spot, rounds, win_cols,
-    features, fine_in, fine_out, cotangent, expand, contract, merge, coarse_in, coarse_out,
-    g1_ref, g2_ref, gm_ref, gc_ref,
+    features, g1_in, fine_in, fine_out, g2_in, expand, contract, gm_in, merge, gc_in, coarse_in, coarse_out, cotangent,
     out_ref, dx_ref, sum_ref,
-    f_ref, fin, fout, cot_ref, we, wc, wm, cin, cout,
+    f_ref, g1_ref, fin, fout, g2_ref, we, wc, gm_ref, wm, gc_ref, cin, cout, cot_ref,
     f_halo, cot_halo, mid_halo, prefix,
     cells, x_ref, qkv_ref, w_ref, ctx_ref, dqkv_ref, d_all,
     mid_ref, dmid_ref, out_frame, dx_frame, coarse_cells, quads, h_ref, act_ref,
@@ -245,19 +246,19 @@
     above, below = (me + n - 1) % n, (me + 1) % n
     last = (me == n - 1).astype(jnp.int32)
 
-    sources = (features, fine_in, fine_out, cotangent, expand, contract, merge, coarse_in, coarse_out)
-    targets = (f_ref, fin, fout, cot_ref, we, wc, wm, cin, cout)
+    ring = Ring(chips, rounds, pack_ref, sum_ref, pair_buf, acc, ring_buf, ring_sems)
+    barrier = pltpu.get_barrier_semaphore()
+    for other in (above, below, ring.ahead, ring.behind, ring.mate):
+        pl.semaphore_signal(barrier, inc=1, device_id={"rows": other}, device_id_type=MESH)
+
+    sources = (features, g1_in, fine_in, fine_out, g2_in, expand, contract, gm_in, merge, gc_in, coarse_in, coarse_out, cotangent)
+    targets = (f_ref, g1_ref, fin, fout, g2_ref, we, wc, gm_ref, wm, gc_ref, cin, cout, cot_ref)
     loads = {
         name: pltpu.make_async_copy(src, dst, load_sem.at[i])
         for i, (name, src, dst) in enumerate(zip(LOADS, sources, targets))
     }
     for name in LOADS:
         loads[name].start()
-
-    ring = Ring(chips, rounds, pack_ref, sum_ref, pair_buf, acc, ring_buf, ring_sems)
-    barrier = pltpu.get_barrier_semaphore()
-    for other in (above, below, ring.ahead, ring.behind, ring.mate):
-        pl.semaphore_signal(barrier, inc=1, device_id={"rows": other}, device_id_type=MESH)
     pl.semaphore_wait(barrier, 5)
 
     def halo(i, src, dst, target):
@@ -274,6 +275,7 @@
 
     cells[...] = jnp.zeros_like(cells)
     quads[...] = jnp.zeros_like(quads)
+    loads["g1"].wait()
     g1 = g1_ref[...].reshape(1, cf)
     rows_per = win_cols * TOK
 
@@ -315,6 +317,8 @@
         if wr == 0:
             send_mid.start()
 
+    for name in ("g2", "gm", "gc"):
+        loads[name].wait()
     g2 = g2_ref[...].reshape(1, cf)
     gmv = gm_ref[...].reshape(1, 4 * cf)
     gm = [gmv[:, k * cf : (k + 1) * cf] for k in range(4)]
@@ -483,12 +487,9 @@
     keep_out.start()
     keep_dx.start()
     count = len(rounds)
-    starts = [0, 1, 2, 3, 5]
     done = [1 + win_rows + 3 - r for r in range(4)] + [0]
     steps = 2 * chips - 1
-    todo = sorted(
-        (s + starts[r], r, s) for r in range(count) for s in range(done[r], steps)
-    )
+    todo = sorted(((s - done[r] + 0.5) / (steps - done[r]), r, s) for r in range(count) for s in range(done[r], steps))
     for _, r, s in todo:
         ring.advance(r, s)
     for r in range(count):
@@ -588,7 +589,8 @@
     scratch = [
         pltpu.VMEM(a.shape, F32)
         for a in (
-            features, fine_project_in, fine_project_out, cotangent, fine_expand, fine_expand, merge_weight, coarse_project_in, coarse_project_out,
+            features, fine_gain_one, fine_project_in, fine_project_out, fine_gain_two, fine_expand, fine_expand,
+            merge_gain, merge_weight, coarse_gain, coarse_project_in, coarse_project_out, cotangent,
         )
     ]
     scratch += [
@@ -625,16 +627,21 @@
     out_slab, dx, summed = pl.pallas_call(
         functools.partial(whole_step, grad_scale, chips, spot, rounds, win_cols),
         out_shape=(shape(low, narrow, cc), shape(height, breadth, cf), shape(total, cc)),
-        in_specs=[anywhere] * 9 + [vmem] * 4,
+        in_specs=[pl.BlockSpec(memory_space=pltpu.HBM)] * len(LOADS),
         out_specs=(vmem,) * 3,
         scratch_shapes=scratch,
         compiler_params=pltpu.CompilerParams(
-            collective_id=0, has_side_effects=True, vmem_limit_bytes=50 * 2**20
+            collective_id=0, has_side_effects=True, vmem_limit_bytes=36 * 2**20
         ),
         name="whole_step",
     )(
-        features, fine_project_in, fine_project_out, cotangent, fine_expand, fine_contract.T, merge_weight, coarse_project_in, coarse_project_out,
-        fine_gain_one, fine_gain_two, merge_gain, coarse_gain,
+        *(
+            pltpu.with_memory_space_constraint(a, pltpu.HBM)
+            for a in (
+                features, fine_gain_one, fine_project_in, fine_project_out, fine_gain_two, fine_expand, fine_contract.T,
+                merge_gain, merge_weight, coarse_gain, coarse_project_in, coarse_project_out, cotangent,
+            )
+        )
     )
     final = pl.pallas_call(
         functools.partial(unpack, spot, cf, cc),

time: 117 us -> 94.9 us (0.81)
  local copies, waits for them, and re-layouts: 12.2 us -> 0 us
  Pallas kernels: 103 us -> 93.9 us
    unnamed x24 -> x0, local copies, waits for them, and re-layouts: 12.2 us -> none
    pallas_call x1, Pallas kernels: 99.7 us -> 90.7 us  [shards(): pl.pallas_call(functools.partial(whole_step, grad_scale, chips, spot, rou...]
where the time goes in v2:
time: 94.9 us; the launch traced here: 94.8 us
  Pallas kernels  93.9 us (99%)
    pallas_call x1, Pallas kernels, shards(): pl.pallas_call(functools.partial(whole_step, grad_scale, chips, spot, rou...  90.7 us
    pallas_call x1, Pallas kernels, shards(): pl.pallas_call(functools.partial(unpack, spot, cf, cc), out_shape=(shape(...  3.22 us

profile of v2, /device:TPU:0, one launch (start us, length us, event | category | flops | bytes accessed | tf_op | source)
XLA Modules:
  0.0 94.8 jit_solution(389806754380147749)
XLA Ops:
  0.6 90.7 %whole_step.1 = (f32[7,7,384]{2,1,0:T(8,128)S(1)}, f32[14,14,192]{2,1,0:T(8,128)S(1)}, f32[3584,384]{1,0:T(8,128)S(1)}) custom-call(f32[14,14,192]{2,1,0:T(8,128)} %features.1, f32[192]{0:T(256)} %g1_in.1, f32[192,576]{1,0:T(8,128)} %fine_in.1, f32[192,192]{1,0:T(8,128)} %fine_out.1, f32[192]{0:T(256)} %g2_in.1, f32[192,768]{1,0:T(8,128)} %expand.1, ...), custom_call_target="tpu_custom_call" | custom-call | tf_op jit(solution)/shard_map/whole_step/pallas_call | solution.py:627
  91.4 3.2 %unpack.1 = (f32[7,7,384]{2,1,0:T(8,128)}, f32[14,14,192]{2,1,0:T(8,128)}, f32[192]{0:T(256)}, f32[192,576]{1,0:T(8,128)}, f32[192,192]{1,0:T(8,128)}, /*index=5...) custom-call(f32[3584,384]{1,0:T(8,128)S(1)} %get-tuple-element.29.su, ...), custom_call_target="tpu_custom_call" | custom-call | tf_op jit(solution)/shard_map/unpack/pallas_call | solution.py:646
